TPU v7x, 32 devices: a whole 2x2x4 slice. The times are simulated.
32 devices in a mesh: op: 4 (over y, x), str: 8 (over z, core).
Axes of the slice: x: 2, y: 2, z: 4, core: 2. Of those that a mesh axis runs over, the one named last changes fastest.
Arguments:
- coeffs: float32 [4096, 4096], P('str'), may hold values from -6 to 6
- previous: float32 [4096, 4096], P('str'), may hold values from -6 to 6
- block_values: bfloat16 [4, 32, 6, 128, 128], P('op'), may hold values from -0.21875 to 0.21875
- block_cols: int32 [4, 32, 6], P('op'), may hold values from 0 to 31, as said below
Outputs:
- advanced: float32 [4096, 4096], P('str')
Inputs may be any that keep to these rules, and one draw needn't show every extreme that they name: For every term k and block row r, block_cols[k, r, 0] equals r and the 6 entries of block_cols[k, r] are distinct.
All inputs are finite; a program needn't handle non-finite values.
Results may differ from a plain program's by a relative error of at most 0.0003.
Values sent between devices are 32-bit elements; how exact they have to be, the bound alone decides.
A program may use at most 192 MiB of HBM per device.

v0:
```python
import math
import jax
import jax.numpy as jnp
from jax import lax
from jax.sharding import PartitionSpec as P

STEPS = 2


def per_device(coeffs, previous, block_values, block_cols):
    local_terms = block_values.shape[0]
    step_scale = 2.0 / math.sqrt(local_terms * lax.axis_size("op"))
    factors = block_values.astype(jnp.float32)
    row_count, full_width = coeffs.shape
    block_size = block_values.shape[-1]
    block_count = full_width // block_size
    slot_count = block_cols.shape[2]
    regrouped = lax.all_to_all(
        previous.reshape(row_count, block_count, block_size),
        "str",
        split_axis=1,
        concat_axis=0,
        tiled=True,
    )
    earlier = regrouped.reshape(full_width, row_count).T
    current = coeffs
    for step_index in range(STEPS):
        column_list = block_cols[0].reshape(-1)
        term_factors = factors[0]
        gathered = jnp.take(
            current.reshape(row_count, block_count, block_size), column_list, axis=1
        )
        gathered = gathered.reshape(row_count, block_count, slot_count, block_size)
        beta_side = jnp.einsum(
            "arjc,rjoc->aro", gathered, term_factors, precision=lax.Precision.HIGHEST
        )
        received = lax.all_to_all(beta_side, "str", split_axis=1, concat_axis=0, tiled=True)
        group_count = received.shape[1]
        item_count = received.shape[2]
        grouped = jnp.take(
            received.reshape(block_count, block_size, group_count, item_count), column_list, axis=0
        )
        grouped = grouped.reshape(block_count, slot_count, block_size, group_count, item_count)
        result = jnp.einsum(
            "rjoc,rjcnm->nmro", term_factors, grouped, precision=lax.Precision.HIGHEST
        )
        moved = result.reshape(group_count, item_count, full_width)
        summed = moved.reshape(row_count, full_width)
        updated = step_scale * lax.psum(summed, "op") - earlier
        earlier, current = (current, updated)
    return current


def solution(mesh):
    placed = (P("str", None), P("str", None), P("op", None, None, None, None), P("op", None, None))
    return jax.shard_map(
        per_device, mesh=mesh, in_specs=placed, out_specs=P("str", None), check_vma=False
    )
```

profile of v0, /device:TPU:0, one launch (start us, length us, event | category | flops | bytes accessed | tf_op | source)
XLA Modules:
  0.0 1236.2 jit_solution(6269851794979325475)
XLA Ops:
  6.5 0.8 copy.25
  7.3 0.1 reshape_squeeze.4
  7.4 9.0 copy.26
  16.4 9.0 copy.27
  25.3 22.2 %gather_fusion = f32[192,512,128]{2,1,0:T(8,128)} fusion(f32[512,32,128]{2,0,1:T(8,128)} %copy.27, s32[1024]{0:T(1024)S(1)} %pad_clamp_fusion), kind=kCustom, calls=%fused_computation.clone | custom fusion | bytes 100664064 | tf_op jit(solution)/shard_map/jit(_take)/gather | solution.py:30
  47.6 34.0 %broadcast_select_fusion.3 = f32[192,512,128]{2,1,0:T(8,128)} fusion(f32[192,512,128]{2,1,0:T(8,128)} %gather_fusion, pred[192]{0:T(512)(128)(4,1)S(1)} %compare_and_fusion), kind=kLoop, calls=%fused_computation.7 | loop fusion | flops 12582912 | bytes 100663488 | tf_op jit(solution)/shard_map/jit(_take)/select_n | solution.py:30
  81.6 30.1 %fusion.8 = f32[512,32,128]{2,0,1:T(8,128)} fusion(f32[512,32,6,128]{3,0,2,1:T(8,128)} %bitcast.92, bf16[1,32,6,128,128]{4,3,2,1,0:T(8,128)(2,1)} %param.10), kind=kOutput, calls=%fused_computation.19 | convolution fusion | flops 19327352832 | bytes 65011712 | tf_op jit(solution)/shard_map/arjc,rjoc->aro/dot_general | solution.py:34
  111.7 6.4 all-to-all-start
  118.1 9.0 copy.31
  127.1 175.0 %all-to-all-done = f32[512,32,128]{2,0,1:T(8,128)} async-done(((f32[512,32,128]{2,0,1:T(8,128)}), f32[512,32,128]{2,0,1:T(8,128)}, u32[]{:S(2)}, u32[]{:S(2)}) %all-to-all-start) | async-done | bytes 8388640 | tf_op jit(solution)/shard_map/all_to_all | solution.py:37
  302.1 4.9 all-to-all-start.1
  307.0 0.0 all-reduce.3.cloned.1.call-start
  307.1 7.7 copy.28
  314.7 22.2 %gather_fusion.1 = f32[192,128,4,128]{3,1,2,0:T(8,128)} fusion(f32[32,128,4,128]{3,1,0,2:T(8,128)} %bitcast.91, s32[1024]{0:T(1024)S(1)} %pad_clamp_fusion), kind=kCustom, calls=%fused_computation.1.clone | custom fusion | bytes 100664064 | tf_op jit(solution)/shard_map/jit(_take)/gather | solution.py:40
  337.0 34.9 %broadcast_select_fusion.1 = f32[192,128,4,128]{3,1,2,0:T(8,128)} fusion(f32[192,128,4,128]{3,1,2,0:T(8,128)} %gather_fusion.1, pred[192]{0:T(512)(128)(4,1)S(1)} %compare_and_fusion), kind=kLoop, calls=%fused_computation.5 | loop fusion | flops 12582912 | bytes 100663488 | tf_op jit(solution)/shard_map/jit(_take)/select_n | solution.py:40
  371.9 48.2 %fusion.14 = f32[4,128,32,128]{3,1,0,2:T(8,128)} fusion(f32[32,6,128,4,128]{4,2,3,1,0:T(8,128)} %bitcast.95, bf16[1,32,6,128,128]{4,3,2,1,0:T(8,128)(2,1)} %param.10), kind=kOutput, calls=%fused_computation.21 | convolution fusion | flops 19327352832 | bytes 65011712 | tf_op jit(solution)/shard_map/rjoc,rjcnm->nmro/dot_general | solution.py:44
  420.1 8.2 copy.30
  428.4 11.7 copy.55
  440.1 0.0 all-reduce.3.cloned.1.call-update
  440.1 0.0 all-reduce.5.cloned.1.call-start
  440.1 50.7 %all-to-all-done.1 = f32[512,32,128]{0,2,1:T(8,128)} async-done(((f32[512,32,128]{0,2,1:T(8,128)}), f32[512,32,128]{0,2,1:T(8,128)}, u32[]{:S(2)}, u32[]{:S(2)}) %all-to-all-start.1) | async-done | bytes 8388640 | tf_op jit(solution)/shard_map/all_to_all | solution.py:18
  490.9 8.4 copy.33
  499.2 11.7 copy.50
  511.0 102.6 %all-reduce.3.cloned.1.call-done = f32[512,4096]{1,0:T(8,128)} async-done(((f32[512,4096]{1,0:T(8,128)}), f32[512,4096]{1,0:T(8,128)}) %all-reduce.3.cloned.1.call-update) | async-done | bytes 8388624 | tf_op jit(solution)/shard_map/psum | solution.py:49
  613.6 11.3 bitcast_subtract_fusion
  624.9 9.0 copy.34
  633.9 8.9 copy.35
  642.8 22.2 %gather_fusion.2 = f32[192,512,128]{2,1,0:T(8,128)} fusion(f32[512,32,128]{2,0,1:T(8,128)} %copy.35, s32[1024]{0:T(1024)S(1)} %pad_clamp_fusion), kind=kCustom, calls=%fused_computation.2.clone | custom fusion | bytes 100664064 | tf_op jit(solution)/shard_map/jit(_take)/gather | solution.py:30
  665.0 34.0 %broadcast_select_fusion.2 = f32[192,512,128]{2,1,0:T(8,128)} fusion(f32[192,512,128]{2,1,0:T(8,128)} %gather_fusion.2, pred[192]{0:T(512)(128)(4,1)S(1)} %compare_and_fusion), kind=kLoop, calls=%fused_computation.6 | loop fusion | flops 12582912 | bytes 100663488 | tf_op jit(solution)/shard_map/jit(_take)/select_n | solution.py:30
  699.1 30.1 %fusion.11 = f32[512,32,128]{2,0,1:T(8,128)} fusion(f32[512,32,6,128]{3,0,2,1:T(8,128)} %bitcast.93, bf16[1,32,6,128,128]{4,3,2,1,0:T(8,128)(2,1)} %param.10), kind=kOutput, calls=%fused_computation.20 | convolution fusion | flops 19327352832 | bytes 65011712 | tf_op jit(solution)/shard_map/arjc,rjoc->aro/dot_general | solution.py:34
  729.2 188.9 %all_to_all.45 = f32[512,32,128]{2,0,1:T(8,128)S(1)} all-to-all(f32[512,32,128]{2,0,1:T(8,128)} %fusion.11), channel_id=1, replica_groups=mesh['op'=4,'str'=8] {'str'}, dimensions={1} | all-to-all | bytes 16777216 | tf_op jit(solution)/shard_map/all_to_all | solution.py:37
  918.1 4.0 copy.36
  922.1 22.2 %gather_fusion.3 = f32[192,128,4,128]{3,1,2,0:T(8,128)} fusion(f32[32,128,4,128]{3,1,0,2:T(8,128)} %bitcast.90, s32[1024]{0:T(1024)S(1)} %pad_clamp_fusion), kind=kCustom, calls=%fused_computation.3.clone | custom fusion | bytes 100664064 | tf_op jit(solution)/shard_map/jit(_take)/gather | solution.py:40
  944.3 34.9 %broadcast_select_fusion = f32[192,128,4,128]{3,1,2,0:T(8,128)} fusion(f32[192,128,4,128]{3,1,2,0:T(8,128)} %gather_fusion.3, pred[192]{0:T(512)(128)(4,1)S(1)} %compare_and_fusion), kind=kLoop, calls=%fused_computation.4 | loop fusion | flops 12582912 | bytes 100663488 | tf_op jit(solution)/shard_map/jit(_take)/select_n | solution.py:40
  979.3 47.8 %fusion.17 = f32[4,128,32,128]{3,1,0,2:T(8,128)} fusion(f32[32,6,128,4,128]{4,2,3,1,0:T(8,128)} %bitcast.94, bf16[1,32,6,128,128]{4,3,2,1,0:T(8,128)(2,1)} %param.10), kind=kOutput, calls=%fused_computation.22 | convolution fusion | flops 19327352832 | bytes 65011712 | tf_op jit(solution)/shard_map/rjoc,rjcnm->nmro/dot_general | solution.py:44
  1027.1 8.2 copy.38
  1035.4 11.8 copy.54
  1047.1 0.0 all-reduce.5.cloned.1.call-update
  1047.1 170.5 %all-reduce.5.cloned.1.call-done = f32[512,4096]{1,0:T(8,128)} async-done(((f32[512,4096]{1,0:T(8,128)}), f32[512,4096]{1,0:T(8,128)}) %all-reduce.5.cloned.1.call-update) | async-done | bytes 8388624 | tf_op jit(solution)/shard_map/psum | solution.py:49
  1217.6 11.3 sub.7
  (3 shorter events, 0.0 us)
Async XLA Ops:
  111.7 190.3 %all-to-all-start = ((f32[512,32,128]{2,0,1:T(8,128)}), f32[512,32,128]{2,0,1:T(8,128)}, u32[]{:S(2)}, u32[]{:S(2)}) async-start(f32[512,32,128]{2,0,1:T(8,128)} %fusion.8), calls=%async_computation | async-start | bytes 16777216 | tf_op jit(solution)/shard_map/all_to_all | solution.py:37
  302.1 188.8 %all-to-all-start.1 = ((f32[512,32,128]{0,2,1:T(8,128)}), f32[512,32,128]{0,2,1:T(8,128)}, u32[]{:S(2)}, u32[]{:S(2)}) async-start(f32[512,32,128]{0,2,1:T(8,128)} %bitcast.97), calls=%async_computation.1 | async-start | bytes 16777216 | tf_op jit(solution)/shard_map/all_to_all | solution.py:18
  307.0 306.5 %all-reduce.3.cloned.1.call-start = ((), (), s32[]{:S(2)}) async-start(), calls=%async_computation.3 | async-start | bytes 16777216 | tf_op jit(solution)/shard_map/psum | solution.py:49
  440.1 777.5 %all-reduce.5.cloned.1.call-start = ((), (), s32[]{:S(2)}) async-start(), calls=%async_computation.4 | async-start | bytes 16777216 | tf_op jit(solution)/shard_map/psum | solution.py:49
Sparse Core Ops, SparseCore 0:
  440.2 173.3 all-reduce.2
  1047.3 170.2 all-reduce.4
where the time goes:
time: 1250 us; the launch traced here: 1240 us
  waiting for transfers between devices  499 us (40%)
  local copies, waits for them, and re-layouts  206 us (16%)
  blocking collectives  189 us (15%)
  other arithmetic  161 us (13%)
  matrix products  156 us (12%)
  between operations  13.9 us (1%)
    psum x2, waiting for transfers between devices, per_device(): updated = step_scale * lax.psum(summed, 'op') - earlier  273 us
    all_to_all x1, blocking collectives, per_device(): lax.all_to_all(beta_side, 'str', split_axis=1, concat_axis=0, tiled=True)  189 us
    all_to_all x1, waiting for transfers between devices, per_device(): lax.all_to_all(beta_side, 'str', split_axis=1, concat_axis=0, tiled=True)  175 us
    dot_general x2, matrix products, per_device(): jnp.einsum('rjoc,rjcnm->nmro', term_factors, grouped, precision=lax.Preci...  96.1 us
    select_n x3, other arithmetic, per_device(): jnp.take(received.reshape(block_count, block_size, group_count, item_coun...  69.9 us
    select_n x2, other arithmetic, per_device(): jnp.take(current.reshape(row_count, block_count, block_size), column_list...  68.1 us
    dot_general x2, matrix products, per_device(): jnp.einsum('arjc,rjoc->aro', gathered, term_factors, precision=lax.Precis...  60.2 us
    unnamed x6, local copies, waits for them, and re-layouts  53.9 us
  transfers between devices with their start and end apart: 4, of which 4 were waited for; matrix products, arithmetic and copies ran while one was open for 13% of the time, Pallas kernels for 0%

commit v1 on v0

--- a/solution.py
+++ b/solution.py
@@ -46,7 +46,7 @@
         )
         moved = result.reshape(group_count, item_count, full_width)
         summed = moved.reshape(row_count, full_width)
-        updated = step_scale * lax.psum(summed, "op") - earlier
+        updated = step_scale * jnp.sum(lax.all_gather(summed, "op"), axis=0) - earlier
         earlier, current = (current, updated)
     return current
 

time: 1250 us -> 1520 us (1.22)
  blocking collectives: 189 us -> 567 us
  waiting for transfers between devices: 499 us -> 377 us
  other arithmetic: 161 us -> 192 us
    all_gather x0 -> x2, waiting for transfers between devices: none -> 377 us  [per_device(): lax.all_gather(summed, 'op')]
    psum x2 -> x0, waiting for transfers between devices: 273 us -> none  [per_device(): updated = step_scale * lax.psum(summed, 'op') - earlier]
    all_to_all x2 -> x0, waiting for transfers between devices: 226 us -> none  [the longest x1 175 us: per_device(): lax.all_to_all(beta_side, 'str', split_axis=1, concat_axis=0, tiled=True)]
    all_to_all x1 -> x2, blocking collectives: 189 us -> 379 us  [per_device(): lax.all_to_all(beta_side, 'str', split_axis=1, concat_axis=0, tiled=True)]
    all_to_all x0 -> x1, blocking collectives: none -> 188 us  [per_device(): lax.all_to_all(previous.reshape(row_count, block_count, block_size), 'str...]
    reduce_sum x0 -> x2, other arithmetic: none -> 31.7 us  [per_device(): jnp.sum(lax.all_gather(summed, 'op'), axis=0)]
    unnamed x6 -> x4, local copies, waits for them, and re-layouts: 53.9 us -> 31.1 us
    another operation x0 -> x2, local copies, waits for them, and re-layouts: none -> 18.7 us  [per_device(): lax.all_gather(summed, 'op')]
  transfers between devices with their start and end apart: 4 -> 2, of which waited for: 4 -> 2; matrix products, arithmetic and copies ran while one was open for 13% -> 2% of each run, Pallas kernels for 0% -> 0%
where the time goes in v1:
time: 1520 us; the launch traced here: 1510 us
  blocking collectives  567 us (37%)
  waiting for transfers between devices  377 us (25%)
  local copies, waits for them, and re-layouts  201 us (13%)
  other arithmetic  192 us (13%)
  matrix products  156 us (10%)
    all_to_all x2, blocking collectives, per_device(): lax.all_to_all(beta_side, 'str', split_axis=1, concat_axis=0, tiled=True)  379 us
    all_gather x2, waiting for transfers between devices, per_device(): lax.all_gather(summed, 'op')  377 us
    all_to_all x1, blocking collectives, per_device(): lax.all_to_all(previous.reshape(row_count, block_count, block_size), 'str...  188 us
    dot_general x2, matrix products, per_device(): jnp.einsum('rjoc,rjcnm->nmro', term_factors, grouped, precision=lax.Preci...  95.9 us
    select_n x3, other arithmetic, per_device(): jnp.take(received.reshape(block_count, block_size, group_count, item_coun...  69.9 us
    select_n x2, other arithmetic, per_device(): jnp.take(current.reshape(row_count, block_count, block_size), column_list...  68.1 us
    dot_general x2, matrix products, per_device(): jnp.einsum('arjc,rjoc->aro', gathered, term_factors, precision=lax.Precis...  60.4 us
    gather x2, local copies, waits for them, and re-layouts, per_device(): jnp.take(current.reshape(row_count, block_count, block_size), column_list...  44.5 us
  transfers between devices with their start and end apart: 2, of which 2 were waited for; matrix products, arithmetic and copies ran while one was open for 2% of the time, Pallas kernels for 0%

profile of v1, /device:TPU:0, one launch (start us, length us, event | category | flops | bytes accessed | tf_op | source)
XLA Modules:
  0.0 1507.7 jit_solution(930858758463494106)
XLA Ops:
  6.5 0.0 all-gather.3.cloned.1.call-start
  6.5 0.8 copy.39
  7.3 0.1 reshape_squeeze.4
  7.4 9.0 copy.40
  16.4 9.0 copy.41
  25.4 22.2 %gather_fusion = f32[192,512,128]{2,1,0:T(8,128)} fusion(f32[512,32,128]{2,0,1:T(8,128)} %copy.41, s32[1024]{0:T(1024)S(1)} %pad_clamp_fusion), kind=kCustom, calls=%fused_computation.clone | custom fusion | bytes 100664064 | tf_op jit(solution)/shard_map/jit(_take)/gather | solution.py:30
  47.6 34.0 %broadcast_select_fusion.3 = f32[192,512,128]{2,1,0:T(8,128)} fusion(f32[192,512,128]{2,1,0:T(8,128)} %gather_fusion, pred[192]{0:T(512)(128)(4,1)S(1)} %compare_and_fusion), kind=kLoop, calls=%fused_computation.7 | loop fusion | flops 12582912 | bytes 100663488 | tf_op jit(solution)/shard_map/jit(_take)/select_n | solution.py:30
  81.6 30.1 %fusion.8 = f32[512,32,128]{2,0,1:T(8,128)} fusion(f32[512,32,6,128]{3,0,2,1:T(8,128)} %bitcast.86, bf16[1,32,6,128,128]{4,3,2,1,0:T(8,128)(2,1)} %param.10), kind=kOutput, calls=%fused_computation.17 | convolution fusion | flops 19327352832 | bytes 65011712 | tf_op jit(solution)/shard_map/arjc,rjoc->aro/dot_general | solution.py:34
  111.8 190.2 %all_to_all.45 = f32[512,32,128]{2,0,1:T(8,128)S(1)} all-to-all(f32[512,32,128]{2,0,1:T(8,128)} %fusion.8), channel_id=1, replica_groups=mesh['op'=4,'str'=8] {'str'}, dimensions={1} | all-to-all | bytes 16777216 | tf_op jit(solution)/shard_map/all_to_all | solution.py:37
  302.0 4.0 copy.42
  305.9 22.2 %gather_fusion.1 = f32[192,128,4,128]{3,1,2,0:T(8,128)} fusion(f32[32,128,4,128]{3,1,0,2:T(8,128)} %bitcast.85, s32[1024]{0:T(1024)S(1)} %pad_clamp_fusion), kind=kCustom, calls=%fused_computation.1.clone | custom fusion | bytes 100664064 | tf_op jit(solution)/shard_map/jit(_take)/gather | solution.py:40
  328.2 34.9 %broadcast_select_fusion.1 = f32[192,128,4,128]{3,1,2,0:T(8,128)} fusion(f32[192,128,4,128]{3,1,2,0:T(8,128)} %gather_fusion.1, pred[192]{0:T(512)(128)(4,1)S(1)} %compare_and_fusion), kind=kLoop, calls=%fused_computation.5 | loop fusion | flops 12582912 | bytes 100663488 | tf_op jit(solution)/shard_map/jit(_take)/select_n | solution.py:40
  363.1 47.8 %fusion.14 = f32[4,128,32,128]{3,1,0,2:T(8,128)} fusion(f32[32,6,128,4,128]{4,2,3,1,0:T(8,128)} %bitcast.89, bf16[1,32,6,128,128]{4,3,2,1,0:T(8,128)(2,1)} %param.10), kind=kOutput, calls=%fused_computation.19 | convolution fusion | flops 19327352832 | bytes 65011712 | tf_op jit(solution)/shard_map/rjoc,rjcnm->nmro/dot_general | solution.py:44
  410.9 11.5 copy.44
  422.4 9.4 all_gather_reshape_reshape.6
  431.7 0.0 all-gather.3.cloned.1.call-update
  431.7 0.0 all-gather.5.cloned.1.call-start
  431.8 9.6 copy.45
  441.4 187.9 %all_to_all.46 = f32[512,32,128]{0,2,1:T(8,128)S(1)} all-to-all(f32[512,32,128]{0,2,1:T(8,128)} %bitcast.97), channel_id=1, replica_groups=mesh['op'=4,'str'=8] {'str'}, dimensions={1} | all-to-all | bytes 16777216 | tf_op jit(solution)/shard_map/all_to_all | solution.py:18
  629.3 4.9 copy.47
  634.2 11.7 copy.63
  645.9 82.0 %all-gather.3.cloned.1.call-done = f32[4,512,4096]{2,1,0:T(8,128)} async-done(((f32[1,512,4096]{2,1,0:T(8,128)}), f32[4,512,4096]{2,1,0:T(8,128)}) %all-gather.3.cloned.1.call-update) | async-done | bytes 33554448 | tf_op jit(solution)/shard_map/all_gather | solution.py:49
  727.8 15.9 %reduce_sum.18 = f32[512,4096]{1,0:T(8,128)} reduce(f32[4,512,4096]{2,1,0:T(8,128)} %all-gather.3.cloned.1.call-done, f32[]{:T(128)} %constant.17.clone.1), dimensions={0}, to_apply=%region_0.3 | reduce | flops 6291456 | bytes 41943044 | tf_op jit(solution)/shard_map/reduce_sum | solution.py:49
  743.7 11.3 bitcast_subtract_fusion
  755.0 9.0 copy.48
  764.0 8.9 copy.49
  773.0 22.2 %gather_fusion.2 = f32[192,512,128]{2,1,0:T(8,128)} fusion(f32[512,32,128]{2,0,1:T(8,128)} %copy.49, s32[1024]{0:T(1024)S(1)} %pad_clamp_fusion), kind=kCustom, calls=%fused_computation.2.clone | custom fusion | bytes 100664064 | tf_op jit(solution)/shard_map/jit(_take)/gather | solution.py:30
  795.2 34.0 %broadcast_select_fusion.2 = f32[192,512,128]{2,1,0:T(8,128)} fusion(f32[192,512,128]{2,1,0:T(8,128)} %gather_fusion.2, pred[192]{0:T(512)(128)(4,1)S(1)} %compare_and_fusion), kind=kLoop, calls=%fused_computation.6 | loop fusion | flops 12582912 | bytes 100663488 | tf_op jit(solution)/shard_map/jit(_take)/select_n | solution.py:30
  829.2 30.3 %fusion.11 = f32[512,32,128]{2,0,1:T(8,128)} fusion(f32[512,32,6,128]{3,0,2,1:T(8,128)} %bitcast.87, bf16[1,32,6,128,128]{4,3,2,1,0:T(8,128)(2,1)} %param.10), kind=kOutput, calls=%fused_computation.18 | convolution fusion | flops 19327352832 | bytes 65011712 | tf_op jit(solution)/shard_map/arjc,rjoc->aro/dot_general | solution.py:34
  859.5 188.5 %all_to_all.47 = f32[512,32,128]{2,0,1:T(8,128)S(1)} all-to-all(f32[512,32,128]{2,0,1:T(8,128)} %fusion.11), channel_id=1, replica_groups=mesh['op'=4,'str'=8] {'str'}, dimensions={1} | all-to-all | bytes 16777216 | tf_op jit(solution)/shard_map/all_to_all | solution.py:37
  1048.0 4.0 copy.50
  1051.9 22.2 %gather_fusion.3 = f32[192,128,4,128]{3,1,2,0:T(8,128)} fusion(f32[32,128,4,128]{3,1,0,2:T(8,128)} %bitcast.84, s32[1024]{0:T(1024)S(1)} %pad_clamp_fusion), kind=kCustom, calls=%fused_computation.3.clone | custom fusion | bytes 100664064 | tf_op jit(solution)/shard_map/jit(_take)/gather | solution.py:40
  1074.2 34.9 %broadcast_select_fusion = f32[192,128,4,128]{3,1,2,0:T(8,128)} fusion(f32[192,128,4,128]{3,1,2,0:T(8,128)} %gather_fusion.3, pred[192]{0:T(512)(128)(4,1)S(1)} %compare_and_fusion), kind=kLoop, calls=%fused_computation.4 | loop fusion | flops 12582912 | bytes 100663488 | tf_op jit(solution)/shard_map/jit(_take)/select_n | solution.py:40
  1109.1 48.1 %fusion.17 = f32[4,128,32,128]{3,1,0,2:T(8,128)} fusion(f32[32,6,128,4,128]{4,2,3,1,0:T(8,128)} %bitcast.88, bf16[1,32,6,128,128]{4,3,2,1,0:T(8,128)(2,1)} %param.10), kind=kOutput, calls=%fused_computation.20 | convolution fusion | flops 19327352832 | bytes 65011712 | tf_op jit(solution)/shard_map/rjoc,rjcnm->nmro/dot_general | solution.py:44
  1157.2 11.5 copy.52
  1168.7 9.4 all_gather_reshape_reshape.7
  1178.0 0.0 all-gather.5.cloned.1.call-update
  1178.0 295.2 %all-gather.5.cloned.1.call-done = f32[4,512,4096]{2,1,0:T(8,128)} async-done(((f32[1,512,4096]{2,1,0:T(8,128)}), f32[4,512,4096]{2,1,0:T(8,128)}) %all-gather.5.cloned.1.call-update) | async-done | bytes 33554448 | tf_op jit(solution)/shard_map/all_gather | solution.py:49
  1473.2 15.9 %reduce_sum.19 = f32[512,4096]{1,0:T(8,128)} reduce(f32[4,512,4096]{2,1,0:T(8,128)} %all-gather.5.cloned.1.call-done, f32[]{:T(128)} %constant.17.clone.1), dimensions={0}, to_apply=%region_1.0 | reduce | flops 6291456 | bytes 41943044 | tf_op jit(solution)/shard_map/reduce_sum | solution.py:49
  1489.1 11.3 sub.7
  (3 shorter events, 0.0 us)
Async XLA Ops:
  6.5 721.3 %all-gather.3.cloned.1.call-start = ((), (), s32[]{:S(2)}) async-start(), calls=%async_computation.3 | async-start | bytes 41943040 | tf_op jit(solution)/shard_map/all_gather | solution.py:49
  431.7 1041.5 %all-gather.5.cloned.1.call-start = ((), (), s32[]{:S(2)}) async-start(), calls=%async_computation.4 | async-start | bytes 41943040 | tf_op jit(solution)/shard_map/all_gather | solution.py:49
Sparse Core Ops, SparseCore 0:
  431.9 295.9 all-gather.2
  1178.1 295.0 all-gather.4
